TPU v7x, 32 devices: a whole 2x2x4 slice. The times are simulated.
32 devices in a mesh: rows: 8 (over z, y), cols: 4 (over x, core).
Axes of the slice: x: 2, y: 2, z: 4, core: 2. Of those that a mesh axis runs over, the one named last changes fastest.
Arguments:
- factor: bfloat16 [4096, 256], P(('rows', 'cols')), may hold values from -0.09375 to 0.09375
- cores: bfloat16 [4, 256, 256], replicated, as said below
- tile_values: bfloat16 [4, 96, 512, 128], P(None, 'rows', 'cols'), may hold values from -56 to 56
- tile_rows: int32 [4, 8, 48], P(None, 'rows', 'cols'), may hold values from 0 to 3
- tile_cols: int32 [4, 8, 48], P(None, 'rows', 'cols'), may hold values from 0 to 7
- tile_counts: int32 [4, 8, 4], P(None, 'rows', 'cols'), may hold values from 3 to 12, as said below
Outputs:
- factor_new: bfloat16 [4096, 256], P(('rows', 'cols'))
- cores_new: float32 [4, 256, 256], replicated
Inputs may be any that keep to these rules, and one draw needn't show every extreme that they name: cores are dominated by their positive diagonals. `tile_counts`: every relation has some device whose 12 slots are all used. `tile_rows`: several slots may name the same tile.
All inputs are finite; a program needn't handle non-finite values.
Results may differ from a plain program's by a relative error of at most 0.0034.
The roundings to bfloat16 on the way count: a program that leaves them out, or rounds other values in their place, can miss the bound.
Values may be sent and summed in bfloat16 or wider, within the bound.
No kernel may reach another device: no remote copies, remote signals or barrier semaphores. Data moves between devices by JAX's collectives and lax.ppermute only.
A program may use at most 128 MiB of HBM per device.

v0:
```python
import jax
import jax.numpy as jnp
from jax import lax
from jax.sharding import PartitionSpec as P

ridge_weight = 0.1


def normal_system(summed_gram_matrix, cores_float32):
    direct_part = jnp.einsum(
        "krs,st,kqt->rq",
        cores_float32,
        summed_gram_matrix,
        cores_float32,
        precision=lax.Precision.HIGHEST,
    )
    reflected_part = jnp.einsum(
        "euh,uc,eca->ha",
        cores_float32,
        summed_gram_matrix,
        cores_float32,
        precision=lax.Precision.HIGHEST,
    )
    return (
        direct_part
        + reflected_part
        + ridge_weight * jnp.eye(summed_gram_matrix.shape[0], dtype=jnp.float32)
    )


def solve_rows(cholesky_lhs, numerator):
    halfway = lax.linalg.triangular_solve(cholesky_lhs, numerator.T, left_side=True, lower=True)
    return lax.linalg.triangular_solve(
        cholesky_lhs, halfway, left_side=True, lower=True, transpose_a=True
    ).T


def whiten(cholesky_new, core_num):
    relations, rank_size, _ = core_num.shape
    stacked = core_num.transpose(1, 0, 2).reshape(rank_size, relations * rank_size)
    halfway = lax.linalg.triangular_solve(cholesky_new, stacked, left_side=True, lower=True)
    flipped = (
        halfway.reshape(rank_size, relations, rank_size)
        .transpose(2, 1, 0)
        .reshape(rank_size, relations * rank_size)
    )
    second = lax.linalg.triangular_solve(cholesky_new, flipped, left_side=True, lower=True)
    return second.reshape(rank_size, relations, rank_size).transpose(1, 2, 0)


def local(factor, cores, tile_values, tile_rows, tile_cols, tile_counts):
    relations, slot_count, tile_size, _ = tile_values.shape
    own_rows, rank_size = factor.shape
    row_ids = tile_rows[:, 0, :]
    col_ids = tile_cols[:, 0, :]
    live_mask = (jnp.arange(slot_count, dtype=jnp.int32)[None, :] < tile_counts[:, 0, :]).astype(
        jnp.float32
    )
    cores_float32 = cores.astype(jnp.float32)
    gram_old = lax.psum(
        jnp.dot(factor.T, factor, preferred_element_type=jnp.float32), ("rows", "cols")
    )
    cholesky_lhs = jnp.linalg.cholesky(normal_system(gram_old, cores_float32))
    col_tiles = lax.all_gather(factor, "rows", axis=0, tiled=True).reshape(-1, tile_size, rank_size)
    col_count = col_tiles.shape[0]
    panel_tiles = lax.axis_size("cols") * own_rows // tile_size
    row_partial = jnp.zeros((panel_tiles, tile_size, relations, rank_size), jnp.float32)
    for relation in range(relations):
        products = jnp.einsum(
            "sij,sjr->sir",
            tile_values[relation],
            col_tiles[col_ids[relation]],
            preferred_element_type=jnp.float32,
        )
        products = products * live_mask[relation][:, None, None]
        row_partial = row_partial.at[row_ids[relation], :, relation].add(products)
    row_partial = row_partial.reshape(panel_tiles * tile_size, relations, rank_size)
    flat_partial = row_partial.reshape(panel_tiles * tile_size, relations * rank_size)
    row_sum = lax.psum_scatter(flat_partial, "cols", scatter_dimension=0, tiled=True)
    direct = row_sum.reshape(own_rows, relations, rank_size)
    numerator = jnp.einsum("eks,kqs->eq", direct, cores_float32, precision=lax.Precision.HIGHEST)
    panel = lax.all_gather(factor, "cols", axis=0, tiled=True)
    rotated = jnp.einsum("pr,krs->pks", panel, cores, preferred_element_type=jnp.float32).astype(
        jnp.bfloat16
    )
    rotated_tiles = rotated.reshape(panel_tiles, tile_size, relations, rank_size)
    col_partial = jnp.zeros((col_count, tile_size, rank_size), jnp.float32)
    for relation in range(relations):
        rotated_selection = rotated_tiles[row_ids[relation], :, relation]
        back_products = jnp.einsum(
            "sij,sir->sjr",
            tile_values[relation],
            rotated_selection,
            preferred_element_type=jnp.float32,
        )
        back_products = back_products * live_mask[relation][:, None, None]
        col_partial = col_partial.at[col_ids[relation]].add(back_products)
    col_partial = col_partial.reshape(col_count * tile_size, rank_size)
    numerator = numerator + lax.psum_scatter(col_partial, "rows", scatter_dimension=0, tiled=True)
    factor_new = solve_rows(cholesky_lhs, numerator).astype(jnp.bfloat16)
    gram_part = jnp.dot(factor_new.T, factor_new, preferred_element_type=jnp.float32)
    col_new = lax.all_gather(factor_new, "rows", axis=0, tiled=True).reshape(
        -1, tile_size, rank_size
    )
    panel_new = lax.all_gather(factor_new, "cols", axis=0, tiled=True).reshape(
        -1, tile_size, rank_size
    )
    core_matrices = []
    for relation in range(relations):
        upper = jnp.einsum(
            "sij,sir->sjr",
            tile_values[relation],
            panel_new[row_ids[relation]],
            preferred_element_type=jnp.float32,
        ).astype(jnp.bfloat16)
        upper = jnp.where(live_mask[relation][:, None, None] > 0, upper, jnp.zeros_like(upper))
        core_matrices.append(
            jnp.einsum(
                "sjr,sjq->rq", upper, col_new[col_ids[relation]], preferred_element_type=jnp.float32
            )
        )
    core_part = jnp.stack(core_matrices, axis=0)
    gram_new = lax.psum(gram_part, ("rows", "cols"))
    core_num = lax.psum(core_part, ("rows", "cols"))
    cores_new = whiten(jnp.linalg.cholesky(gram_new), core_num)
    return (factor_new, cores_new)


def solution(mesh):
    in_specs = (
        P(("rows", "cols"), None),
        P(),
        P(None, "rows", "cols", None),
        P(None, "rows", "cols"),
        P(None, "rows", "cols"),
        P(None, "rows", "cols"),
    )
    out_specs = (P(("rows", "cols"), None), P())
    return jax.shard_map(local, mesh=mesh, in_specs=in_specs, out_specs=out_specs, check_vma=False)
```

profile of v0, /device:TPU:0, one launch (start us, length us, event | category | flops | bytes accessed | tf_op | source)
XLA Modules:
  0.0 483.6 jit_solution(10696427226409059928)
XLA Ops:
  8.1 1.9 fusion.113
  10.0 33.4 %all_gather.12 = bf16[1024,256]{1,0:T(8,128)(2,1)S(1)} all-gather(bf16[128,256]{1,0:T(8,128)(2,1)} %param.9), channel_id=1, replica_groups=mesh['rows'=8,'cols'=4] {'rows'}, dimensions={0}, use_global_device_ids=true | all-gather | bytes 589824 | tf_op jit(solution)/shard_map/all_gather | solution.py:64
  45.6 1.5 gather_fusion
  47.1 1.5 gather_fusion.1
  48.6 1.5 gather_fusion.2
  50.8 1.8 multiply_bitcast_fusion.7
  52.7 1.6 multiply_bitcast_fusion.6
  54.3 1.6 multiply_bitcast_fusion.5
  55.9 1.6 multiply_bitcast_fusion.4
  57.4 1.6 copy.35
  59.0 3.1 copy.37
  62.2 1.6 copy.39
  63.8 3.0 copy.41
  67.1 3.2 scatter_fusion
  70.2 3.2 scatter_fusion.1
  73.4 3.2 scatter_fusion.2
  76.6 3.2 scatter_fusion.3
  81.1 1.8 copy.97
  83.8 6.0 %all_gather.13 = bf16[512,256]{1,0:T(8,128)(2,1)S(1)} all-gather(bf16[128,256]{1,0:T(8,128)(2,1)S(1)} %copy-done.9), channel_id=1, replica_groups=mesh['rows'=8,'cols'=4] {'cols'}, dimensions={0}, use_global_device_ids=true | all-gather | bytes 327680 | tf_op jit(solution)/shard_map/all_gather | solution.py:82
  90.9 2.7 multiply_bitcast_fusion.3
  93.6 1.9 copy.47
  95.5 1.5 gather_fusion.5
  97.0 2.8 multiply_bitcast_fusion.2
  99.8 3.1 copy.50
  103.0 1.5 gather_fusion.6
  104.5 2.9 multiply_bitcast_fusion.1
  107.4 3.1 copy.53
  110.4 1.5 gather_fusion.7
  111.9 2.8 multiply_bitcast_fusion
  114.7 3.1 copy.56
  117.9 1.8 scatter_fusion.4
  119.8 3.1 scatter_fusion.5
  122.9 1.8 scatter_fusion.6
  124.8 3.1 scatter_fusion.7
  129.5 22.2 %all-reduce.9.cloned.1.call-done = f32[256,256]{1,0:T(8,128)} async-done(((f32[256,256]{1,0:T(8,128)}), f32[256,256]{1,0:T(8,128)}) %all-reduce.9.cloned.1.call-update) | async-done | bytes 262160 | tf_op jit(solution)/shard_map/psum | solution.py:60
  151.7 1.7 fusion.67
  155.7 11.7 %cholesky.130 = f32[128,128]{1,0:T(8,128)S(1)} custom-call(f32[128,128]{1,0:T(8,128)S(1)} %cholesky.194), custom_call_target="Cholesky" | custom-call | tf_op jit(solution)/shard_map/jit(cholesky)/cholesky | solution.py:63
  167.6 9.8 %custom-call.35 = f32[1,128,128]{1,2,0:T(8,128)S(1)} custom-call(f32[1,128,128]{2,1,0:T(8,128)S(1)} %get-tuple-element.75), custom_call_target="InvertDiagBlocksLowerTriangular" | custom-call | tf_op jit(solution)/shard_map/jit(cholesky)/cholesky | solution.py:63
  178.0 11.9 %cholesky.147 = f32[128,128]{1,0:T(8,128)S(1)} custom-call(f32[128,128]{1,0:T(8,128)S(1)} %convolution_subtract_fusion.5), custom_call_target="Cholesky" | custom-call | tf_op jit(solution)/shard_map/jit(cholesky)/cholesky | solution.py:63
  192.2 4.4 while.5
  196.6 19.7 %custom-call.16 = f32[2,128,128]{1,2,0:T(8,128)S(1)} custom-call(f32[2,128,128]{2,1,0:T(8,128)S(1)} %get-tuple-element.19), custom_call_target="InvertDiagBlocksLowerTriangular" | custom-call | tf_op jit(solution)/shard_map/triangular_solve | solution.py:33
  217.6 1.5 fusion.19
  221.5 27.7 %all_gather.15 = bf16[1024,256]{0,1:T(8,128)(2,1)S(1)} all-gather(bf16[128,256]{0,1:T(8,128)(2,1)S(1)} %fusion.88), channel_id=1, replica_groups=mesh['rows'=8,'cols'=4] {'rows'}, dimensions={0}, use_global_device_ids=true | all-gather | bytes 589824 | tf_op jit(solution)/shard_map/all_gather | solution.py:102
  249.2 5.8 %all_gather.14 = bf16[512,256]{0,1:T(8,128)(2,1)S(1)} all-gather(bf16[128,256]{0,1:T(8,128)(2,1)S(1)} %fusion.88), channel_id=1, replica_groups=mesh['rows'=8,'cols'=4] {'cols'}, dimensions={0}, use_global_device_ids=true | all-gather | bytes 327680 | tf_op jit(solution)/shard_map/all_gather | solution.py:105
  255.2 1.5 gather_fusion.9
  256.7 1.5 gather_fusion.11
  258.2 1.5 gather_fusion.13
  260.4 1.5 gather_fusion.8
  261.9 1.5 gather_fusion.10
  263.4 1.5 gather_fusion.12
  265.0 1.5 gather_fusion.14
  266.5 2.1 fusion.12
  268.5 2.1 fusion.13
  270.6 2.8 fusion.14
  273.4 2.5 fusion.15
  275.9 2.1 pad_maximum_fusion
  278.7 128.2 %all-reduce.11.cloned.1.call-done = (f32[256,1024]{0,1:T(8,128)}, f32[256,256]{0,1:T(8,128)}) async-done(((f32[256,1024]{0,1:T(8,128)}, f32[256,256]{0,1:T(8,128)}), (f32[256,1024]{0,1:T(8,128)}, f32[256,256]{0,1:T(8,128)})) %all-reduce.11.cloned.1.call-update) | async-done | bytes 1310736 | tf_op jit(solution)/shard_map/psum | solution.py:124
  409.0 11.7 %cholesky.164 = f32[128,128]{1,0:T(8,128)S(1)} custom-call(f32[128,128]{1,0:T(8,128)S(1)} %cholesky.197), custom_call_target="Cholesky" | custom-call | tf_op jit(solution)/shard_map/jit(cholesky)/cholesky | solution.py:125
  420.8 9.8 %custom-call.36 = f32[1,128,128]{1,2,0:T(8,128)S(1)} custom-call(f32[1,128,128]{2,1,0:T(8,128)S(1)} %get-tuple-element.73), custom_call_target="InvertDiagBlocksLowerTriangular" | custom-call | tf_op jit(solution)/shard_map/jit(cholesky)/cholesky | solution.py:125
  431.1 11.9 %cholesky.181 = f32[128,128]{1,0:T(8,128)S(1)} custom-call(f32[128,128]{1,0:T(8,128)S(1)} %convolution_subtract_fusion.2), custom_call_target="Cholesky" | custom-call | tf_op jit(solution)/shard_map/jit(cholesky)/cholesky | solution.py:125
  445.7 4.1 while.6
  446.4 1.4 bitcast_dynamic-update-slice_fusion.5
  448.4 1.4 bitcast_dynamic-update-slice_fusion.5
  449.8 19.7 %custom-call.38 = f32[2,128,128]{1,2,0:T(8,128)S(1)} custom-call(f32[2,128,128]{2,1,0:T(8,128)S(1)} %get-tuple-element.27), custom_call_target="InvertDiagBlocksLowerTriangular" | custom-call | tf_op jit(solution)/shard_map/triangular_solve/custom-call.5 | solution.py:47
  (124 shorter events, 33.1 us)
Async XLA Ops:
  8.0 81.8 %copy-start = (bf16[4,256,256]{2,1,0:T(8,128)(2,1)S(1)}, bf16[4,256,256]{2,1,0:T(8,128)(2,1)}, u32[]{:S(2)}) copy-start(bf16[4,256,256]{2,1,0:T(8,128)(2,1)} %param.10) | copy-start | bytes 1572868
  8.0 143.7 %all-reduce.9.cloned.1.call-start = ((), (), s32[]{:S(2)}) async-start(), calls=%async_computation.2 | async-start | bytes 524288 | tf_op jit(solution)/shard_map/psum | solution.py:60
  9.9 206.4 %reduce-scatter.3.cloned.1.call-start = ((), (), s32[]{:S(2)}) async-start(), calls=%async_computation.3 | async-start | bytes 2621440 | tf_op jit(solution)/shard_map/reduce_scatter | solution.py:79
  50.7 1.8 copy-start.4
  50.8 2.0 copy-start.6
  52.6 1.7 copy-start.7
  59.0 3.1 copy-start.3
  82.9 0.8 copy-start.9
  82.9 134.6 %reduce-scatter.5.cloned.1.call-start = ((), (), s32[]{:S(2)}) async-start(), calls=%async_computation.4 | async-start | bytes 1179648 | tf_op jit(solution)/shard_map/reduce_scatter | solution.py:99
  119.8 3.1 copy-start.2
  127.9 1.0 copy-start.1
  128.9 278.0 %all-reduce.11.cloned.1.call-start = ((), (), s32[]{:S(2)}) async-start(), calls=%async_computation.5 | async-start | bytes 2621440 | tf_op jit(solution)/shard_map/psum | solution.py:124
  151.7 2.5 copy-start.8
  263.4 3.0 copy-start.5
  409.0 60.6 %copy-start.10 = (f32[256,1024]{0,1:T(8,128)S(1)}, f32[256,1024]{0,1:T(8,128)}, u32[]{:S(2)}) copy-start(f32[256,1024]{0,1:T(8,128)} %get-tuple-element.56) | copy-start | bytes 3145732
Sparse Core Ops, SparseCore 0:
  14.3 137.2 all-reduce.8
  278.1 128.7 all-reduce.10
Sparse Core Ops, SparseCore 1:
  83.0 32.4 reduce-scatter.2
  129.0 64.6 reduce-scatter.4
where the time goes:
time: 492 us; the launch traced here: 484 us
  waiting for transfers between devices  150 us (30%)
  other arithmetic  137 us (28%)
  blocking collectives  72.9 us (15%)
  local copies, waits for them, and re-layouts  61.2 us (12%)
  matrix products  42.5 us (9%)
  between operations  19.3 us (4%)
    psum x1, waiting for transfers between devices, local(): core_num = lax.psum(core_part, ('rows', 'cols'))  128 us
    another operation x7, other arithmetic, local(): cores_new = whiten(jnp.linalg.cholesky(gram_new), core_num)  34.8 us
    another operation x6, other arithmetic, local(): cholesky_lhs = jnp.linalg.cholesky(normal_system(gram_old, cores_float32))  34.2 us
    all_gather x1, blocking collectives, local(): lax.all_gather(factor, 'rows', axis=0, tiled=True)  33.4 us
    all_gather x1, blocking collectives, local(): lax.all_gather(factor_new, 'rows', axis=0, tiled=True)  27.7 us
    psum x1, waiting for transfers between devices, local(): lax.psum(jnp.dot(factor.T, factor, preferred_element_type=jnp.float32), (...  22.2 us
    another operation x3, other arithmetic, whiten(): lax.linalg.triangular_solve(cholesky_new, flipped, left_side=True, lower=...  19.8 us
    another operation x3, other arithmetic, solve_rows(): lax.linalg.triangular_solve(cholesky_lhs, halfway, left_side=True, lower=...  19.7 us
  transfers between devices with their start and end apart: 4, of which 2 were waited for; matrix products, arithmetic and copies ran while one was open for 29% of the time, Pallas kernels for 0%

commit v1 on v0

--- a/solution.py
+++ b/solution.py
@@ -1,9 +1,37 @@
+import functools
 import jax
 import jax.numpy as jnp
 from jax import lax
 from jax.sharding import PartitionSpec as P
 
 ridge_weight = 0.1
+
+
+def store_strips_all_all(values, dim_at):
+    seen_now = lax.axis_size("rows")
+    after, finding, back = (seen_now, lax.axis_index("rows"), values.shape[dim_at])
+    series = [rr * after if dev_j == dim_at else rr for dev_j, rr in enumerate(values.shape)]
+    left_arr = jnp.zeros(series, values.dtype)
+    w1 = lax.dynamic_update_slice_in_dim(left_arr, values, finding * back, axis=dim_at)
+    t_next = x_next = values
+    for q in range(1, after // 2 + 1):
+        t_next = lax.ppermute(
+            t_next,
+            axis_name="rows",
+            perm=list(map(lambda dev_j: (dev_j, (dev_j + 1) % after), range(after))),
+        )
+        w1 = lax.dynamic_update_slice_in_dim(w1, t_next, (finding - q) % after * back, axis=dim_at)
+        if 2 * q < after:
+            x_next = lax.ppermute(
+                x_next, "rows", list(map(lambda dev_j: (dev_j, (dev_j - 1) % after), range(after)))
+            )
+            w1 = lax.dynamic_update_slice_in_dim(
+                w1, x_next, (finding + q) % after * back, axis=dim_at
+            )
+    return w1
+
+
+words_raise = functools.partial(store_strips_all_all, dim_at=0)
 
 
 def normal_system(summed_gram_matrix, cores_float32):
@@ -61,7 +89,7 @@
         jnp.dot(factor.T, factor, preferred_element_type=jnp.float32), ("rows", "cols")
     )
     cholesky_lhs = jnp.linalg.cholesky(normal_system(gram_old, cores_float32))
-    col_tiles = lax.all_gather(factor, "rows", axis=0, tiled=True).reshape(-1, tile_size, rank_size)
+    col_tiles = words_raise(factor).reshape(-1, tile_size, rank_size)
     col_count = col_tiles.shape[0]
     panel_tiles = lax.axis_size("cols") * own_rows // tile_size
     row_partial = jnp.zeros((panel_tiles, tile_size, relations, rank_size), jnp.float32)

time: 492 us -> 484 us (0.984)
  blocking collectives: 72.9 us -> 39.6 us
  starting transfers between devices: 0.63 us -> 16.2 us
  waiting for transfers between devices: 150 us -> 159 us
    all_gather x1 -> x0, blocking collectives: 33.4 us -> none  [local(): lax.all_gather(factor, 'rows', axis=0, tiled=True)]
    ppermute x0 -> x7, starting transfers between devices: none -> 15.6 us  [the longest x3 12.5 us: store_strips_all_all(): lax.ppermute(x_next, 'rows', list(map(lambda dev_j: (dev_j, (dev_j - 1) %...]
    ppermute x0 -> x7, waiting for transfers between devices: none -> 11.5 us  [the longest x4 11.5 us: store_strips_all_all(): lax.ppermute(t_next, axis_name='rows', perm=list(map(lambda dev_j: (dev_j...]
  transfers between devices with their start and end apart: 4 -> 11, of which waited for: 2 -> 5; matrix products, arithmetic and copies ran while one was open for 29% -> 31% of each run, Pallas kernels for 0% -> 0%
where the time goes in v1:
time: 484 us; the launch traced here: 475 us
  waiting for transfers between devices  159 us (33%)
  other arithmetic  137 us (28%)
  local copies, waits for them, and re-layouts  61.8 us (13%)
  matrix products  42.6 us (9%)
  blocking collectives  39.6 us (8%)
  between operations  19.4 us (4%)
  starting transfers between devices  16.2 us (3%)
    psum x1, waiting for transfers between devices, local(): core_num = lax.psum(core_part, ('rows', 'cols'))  128 us
    another operation x7, other arithmetic, local(): cores_new = whiten(jnp.linalg.cholesky(gram_new), core_num)  34.8 us
    another operation x6, other arithmetic, local(): cholesky_lhs = jnp.linalg.cholesky(normal_system(gram_old, cores_float32))  34.1 us
    all_gather x1, blocking collectives, local(): lax.all_gather(factor_new, 'rows', axis=0, tiled=True)  27.6 us
    another operation x3, other arithmetic, whiten(): lax.linalg.triangular_solve(cholesky_new, flipped, left_side=True, lower=...  19.8 us
    another operation x3, other arithmetic, solve_rows(): lax.linalg.triangular_solve(cholesky_lhs, halfway, left_side=True, lower=...  19.7 us
    psum x1, waiting for transfers between devices, local(): lax.psum(jnp.dot(factor.T, factor, preferred_element_type=jnp.float32), (...  18.8 us
    scatter-add x4, other arithmetic, local(): row_partial = row_partial.at[row_ids[relation], :, relation].add(products)  12.7 us
  transfers between devices with their start and end apart: 11, of which 5 were waited for; matrix products, arithmetic and copies ran while one was open for 31% of the time, Pallas kernels for 0%

profile of v1, /device:TPU:0, one launch (start us, length us, event | category | flops | bytes accessed | tf_op | source)
XLA Modules:
  0.0 474.9 jit_solution(16954778751375568869)
XLA Ops:
  8.1 3.0 collective-permute-start
  11.1 3.1 collective-permute-start.1
  14.2 1.8 fusion.113
  19.4 4.7 collective-permute-start.3
  24.1 2.3 collective-permute-done.2
  26.4 4.7 collective-permute-start.5
  31.2 2.3 collective-permute-done.4
  33.5 7.0 %collective-permute-done.6 = bf16[128,256]{1,0:T(8,128)(2,1)S(1)} collective-permute-done((bf16[128,256]{1,0:T(8,128)(2,1)S(1)}, bf16[128,256]{1,0:T(8,128)(2,1)S(1)}, u32[]{:S(2)}, u32[]{:S(2)}) %collective-permute-start.6) | collective-permute-done | bytes 65568 | tf_op jit(solution)/shard_map/ppermute | solution.py:18
  40.5 1.5 gather_fusion
  42.0 1.5 gather_fusion.1
  45.6 1.8 multiply_bitcast_fusion.7
  47.6 1.6 multiply_bitcast_fusion.6
  49.2 1.6 multiply_bitcast_fusion.5
  50.7 1.6 multiply_bitcast_fusion.4
  52.3 1.6 copy.35
  53.9 3.2 copy.37
  57.1 1.6 copy.39
  58.7 3.0 copy.41
  61.9 3.2 scatter_fusion
  65.1 3.2 scatter_fusion.1
  68.3 3.2 scatter_fusion.2
  71.5 3.2 scatter_fusion.3
  76.0 1.8 copy.97
  78.6 6.0 %all_gather.9 = bf16[512,256]{1,0:T(8,128)(2,1)S(1)} all-gather(bf16[128,256]{1,0:T(8,128)(2,1)S(1)} %copy-done.9), channel_id=1, replica_groups=mesh['rows'=8,'cols'=4] {'cols'}, dimensions={0}, use_global_device_ids=true | all-gather | bytes 327680 | tf_op jit(solution)/shard_map/all_gather | solution.py:110
  85.8 2.6 multiply_bitcast_fusion.3
  88.4 1.9 copy.47
  90.3 1.5 gather_fusion.5
  91.8 3.0 multiply_bitcast_fusion.2
  94.8 3.0 copy.50
  97.9 1.5 gather_fusion.6
  99.4 2.9 multiply_bitcast_fusion.1
  102.2 3.1 copy.53
  105.3 1.5 gather_fusion.7
  106.8 2.8 multiply_bitcast_fusion
  109.6 3.1 copy.56
  112.8 1.8 scatter_fusion.4
  114.6 3.1 scatter_fusion.5
  117.8 1.8 scatter_fusion.6
  119.6 3.1 scatter_fusion.7
  124.3 18.8 %all-reduce.9.cloned.1.call-done = f32[256,256]{1,0:T(8,128)} async-done(((f32[256,256]{1,0:T(8,128)}), f32[256,256]{1,0:T(8,128)}) %all-reduce.9.cloned.1.call-update) | async-done | bytes 262160 | tf_op jit(solution)/shard_map/psum | solution.py:88
  143.1 1.7 fusion.67
  147.1 11.7 %cholesky.130 = f32[128,128]{1,0:T(8,128)S(1)} custom-call(f32[128,128]{1,0:T(8,128)S(1)} %cholesky.194), custom_call_target="Cholesky" | custom-call | tf_op jit(solution)/shard_map/jit(cholesky)/cholesky | solution.py:91
  159.0 9.8 %custom-call.35 = f32[1,128,128]{1,2,0:T(8,128)S(1)} custom-call(f32[1,128,128]{2,1,0:T(8,128)S(1)} %get-tuple-element.75), custom_call_target="InvertDiagBlocksLowerTriangular" | custom-call | tf_op jit(solution)/shard_map/jit(cholesky)/cholesky | solution.py:91
  169.4 11.8 %cholesky.147 = f32[128,128]{1,0:T(8,128)S(1)} custom-call(f32[128,128]{1,0:T(8,128)S(1)} %convolution_subtract_fusion.5), custom_call_target="Cholesky" | custom-call | tf_op jit(solution)/shard_map/jit(cholesky)/cholesky | solution.py:91
  183.5 4.2 while.5
  187.8 19.7 %custom-call.16 = f32[2,128,128]{1,2,0:T(8,128)S(1)} custom-call(f32[2,128,128]{2,1,0:T(8,128)S(1)} %get-tuple-element.19), custom_call_target="InvertDiagBlocksLowerTriangular" | custom-call | tf_op jit(solution)/shard_map/triangular_solve | solution.py:61
  212.7 27.6 %all_gather.11 = bf16[1024,256]{0,1:T(8,128)(2,1)S(1)} all-gather(bf16[128,256]{0,1:T(8,128)(2,1)S(1)} %fusion.88), channel_id=1, replica_groups=mesh['rows'=8,'cols'=4] {'rows'}, dimensions={0}, use_global_device_ids=true | all-gather | bytes 589824 | tf_op jit(solution)/shard_map/all_gather | solution.py:130
  240.3 5.9 %all_gather.10 = bf16[512,256]{0,1:T(8,128)(2,1)S(1)} all-gather(bf16[128,256]{0,1:T(8,128)(2,1)S(1)} %fusion.88), channel_id=1, replica_groups=mesh['rows'=8,'cols'=4] {'cols'}, dimensions={0}, use_global_device_ids=true | all-gather | bytes 327680 | tf_op jit(solution)/shard_map/all_gather | solution.py:133
  246.4 1.5 gather_fusion.9
  247.9 1.5 gather_fusion.11
  251.7 1.5 gather_fusion.8
  253.2 1.5 gather_fusion.10
  254.7 1.5 gather_fusion.12
  257.7 2.1 fusion.12
  259.8 2.1 fusion.13
  261.8 2.8 fusion.14
  264.6 2.5 fusion.15
  267.1 2.1 pad_maximum_fusion
  270.0 128.2 %all-reduce.11.cloned.1.call-done = (f32[256,1024]{0,1:T(8,128)}, f32[256,256]{0,1:T(8,128)}) async-done(((f32[256,1024]{0,1:T(8,128)}, f32[256,256]{0,1:T(8,128)}), (f32[256,1024]{0,1:T(8,128)}, f32[256,256]{0,1:T(8,128)})) %all-reduce.11.cloned.1.call-update) | async-done | bytes 1310736 | tf_op jit(solution)/shard_map/psum | solution.py:152
  400.3 11.7 %cholesky.164 = f32[128,128]{1,0:T(8,128)S(1)} custom-call(f32[128,128]{1,0:T(8,128)S(1)} %cholesky.197), custom_call_target="Cholesky" | custom-call | tf_op jit(solution)/shard_map/jit(cholesky)/cholesky | solution.py:153
  412.0 9.8 %custom-call.36 = f32[1,128,128]{1,2,0:T(8,128)S(1)} custom-call(f32[1,128,128]{2,1,0:T(8,128)S(1)} %get-tuple-element.73), custom_call_target="InvertDiagBlocksLowerTriangular" | custom-call | tf_op jit(solution)/shard_map/jit(cholesky)/cholesky | solution.py:153
  422.3 11.9 %cholesky.181 = f32[128,128]{1,0:T(8,128)S(1)} custom-call(f32[128,128]{1,0:T(8,128)S(1)} %convolution_subtract_fusion.2), custom_call_target="Cholesky" | custom-call | tf_op jit(solution)/shard_map/jit(cholesky)/cholesky | solution.py:153
  437.0 4.1 while.6
  441.1 19.7 %custom-call.38 = f32[2,128,128]{1,2,0:T(8,128)S(1)} custom-call(f32[2,128,128]{2,1,0:T(8,128)S(1)} %get-tuple-element.27), custom_call_target="InvertDiagBlocksLowerTriangular" | custom-call | tf_op jit(solution)/shard_map/triangular_solve/custom-call.5 | solution.py:75
  (146 shorter events, 42.8 us)
Async XLA Ops:
  8.0 76.7 %copy-start = (bf16[4,256,256]{2,1,0:T(8,128)(2,1)S(1)}, bf16[4,256,256]{2,1,0:T(8,128)(2,1)}, u32[]{:S(2)}) copy-start(bf16[4,256,256]{2,1,0:T(8,128)(2,1)} %param.10) | copy-start | bytes 1572868
  8.0 135.1 %all-reduce.9.cloned.1.call-start = ((), (), s32[]{:S(2)}) async-start(), calls=%async_computation.2 | async-start | bytes 524288 | tf_op jit(solution)/shard_map/psum | solution.py:88
  8.1 11.3 %collective-permute-start = (bf16[128,256]{1,0:T(8,128)(2,1)}, bf16[128,256]{1,0:T(8,128)(2,1)S(1)}, u32[]{:S(2)}, u32[]{:S(2)}) collective-permute-start(bf16[128,256]{1,0:T(8,128)(2,1)} %param.9), channel_id=1, source_target_pairs={{0,4},{4,8},{8,12},{12,16},{16,20},{20,24},{24,28},{28,0},{1,5},{5... | collective-permute-start | bytes 196616 | tf_op jit(solution)/shard_map/ppermute | solution.py:18
  11.1 8.3 %collective-permute-start.1 = (bf16[128,256]{1,0:T(8,128)(2,1)}, bf16[128,256]{1,0:T(8,128)(2,1)S(1)}, u32[]{:S(2)}, u32[]{:S(2)}) collective-permute-start(bf16[128,256]{1,0:T(8,128)(2,1)} %param.9), channel_id=1, source_target_pairs={{0,28},{4,0},{8,4},{12,8},{16,12},{20,16},{24,20},{28,24},{1,29},{... | collective-permute-start | bytes 196616 | tf_op jit(solution)/shard_map/ppermute | solution.py:25
  16.0 191.4 %reduce-scatter.3.cloned.1.call-start = ((), (), s32[]{:S(2)}) async-start(), calls=%async_computation.3 | async-start | bytes 2621440 | tf_op jit(solution)/shard_map/reduce_scatter | solution.py:107
  19.3 7.1 %collective-permute-start.2 = (bf16[128,256]{1,0:T(8,128)(2,1)S(1)}, bf16[128,256]{1,0:T(8,128)(2,1)S(1)}, u32[]{:S(2)}, u32[]{:S(2)}) collective-permute-start(bf16[128,256]{1,0:T(8,128)(2,1)S(1)} %collective-permute-done), channel_id=1, source_target_pairs={{0,4},{4,8},{8,12},{12,16},{16,20},{20,24},{24,28},{28,0},{1,5},{5... | collective-permute-start | bytes 196616 | tf_op jit(solution)/shard_map/ppermute | solution.py:18
  19.4 7.0 %collective-permute-start.3 = (bf16[128,256]{1,0:T(8,128)(2,1)S(1)}, bf16[128,256]{1,0:T(8,128)(2,1)S(1)}, u32[]{:S(2)}, u32[]{:S(2)}) collective-permute-start(bf16[128,256]{1,0:T(8,128)(2,1)S(1)} %collective-permute-done.1), channel_id=1, source_target_pairs={{0,28},{4,0},{8,4},{12,8},{16,12},{20,16},{24,20},{28,24},{1,29},{... | collective-permute-start | bytes 196616 | tf_op jit(solution)/shard_map/ppermute | solution.py:25
  26.4 7.0 %collective-permute-start.4 = (bf16[128,256]{1,0:T(8,128)(2,1)S(1)}, bf16[128,256]{1,0:T(8,128)(2,1)S(1)}, u32[]{:S(2)}, u32[]{:S(2)}) collective-permute-start(bf16[128,256]{1,0:T(8,128)(2,1)S(1)} %collective-permute-done.2), channel_id=1, source_target_pairs={{0,4},{4,8},{8,12},{12,16},{16,20},{20,24},{24,28},{28,0},{1,5},{5... | collective-permute-start | bytes 196616 | tf_op jit(solution)/shard_map/ppermute | solution.py:18
  26.4 7.0 %collective-permute-start.5 = (bf16[128,256]{1,0:T(8,128)(2,1)S(1)}, bf16[128,256]{1,0:T(8,128)(2,1)S(1)}, u32[]{:S(2)}, u32[]{:S(2)}) collective-permute-start(bf16[128,256]{1,0:T(8,128)(2,1)S(1)} %collective-permute-done.3), channel_id=1, source_target_pairs={{0,28},{4,0},{8,4},{12,8},{16,12},{20,16},{24,20},{28,24},{1,29},{... | collective-permute-start | bytes 196616 | tf_op jit(solution)/shard_map/ppermute | solution.py:25
  33.4 7.0 %collective-permute-start.6 = (bf16[128,256]{1,0:T(8,128)(2,1)S(1)}, bf16[128,256]{1,0:T(8,128)(2,1)S(1)}, u32[]{:S(2)}, u32[]{:S(2)}) collective-permute-start(bf16[128,256]{1,0:T(8,128)(2,1)S(1)} %collective-permute-done.4), channel_id=1, source_target_pairs={{0,4},{4,8},{8,12},{12,16},{16,20},{20,24},{24,28},{28,0},{1,5},{5... | collective-permute-start | bytes 196616 | tf_op jit(solution)/shard_map/ppermute | solution.py:18
  45.6 1.8 copy-start.4
  45.6 2.0 copy-start.7
  47.5 1.7 copy-start.6
  53.9 3.2 copy-start.3
  77.8 0.8 copy-start.9
  77.8 130.9 %reduce-scatter.5.cloned.1.call-start = ((), (), s32[]{:S(2)}) async-start(), calls=%async_computation.4 | async-start | bytes 1179648 | tf_op jit(solution)/shard_map/reduce_scatter | solution.py:127
  114.6 3.1 copy-start.2
  122.8 1.0 copy-start.1
  123.7 274.4 %all-reduce.11.cloned.1.call-start = ((), (), s32[]{:S(2)}) async-start(), calls=%async_computation.5 | async-start | bytes 2621440 | tf_op jit(solution)/shard_map/psum | solution.py:152
  143.1 2.5 copy-start.8
  254.7 3.0 copy-start.5
  400.2 60.6 %copy-start.10 = (f32[256,1024]{0,1:T(8,128)S(1)}, f32[256,1024]{0,1:T(8,128)}, u32[]{:S(2)}) copy-start(f32[256,1024]{0,1:T(8,128)} %get-tuple-element.56) | copy-start | bytes 3145732
Sparse Core Ops, SparseCore 0:
  16.2 126.8 all-reduce.8
  269.3 128.7 all-reduce.10
Sparse Core Ops, SparseCore 1:
  77.9 28.8 reduce-scatter.2
  123.8 61.2 reduce-scatter.4
